TPU v7x, 256 devices: a whole 4x4x8 slice. The times are simulated.
256 devices in a mesh: seq: 32 (over y, x, core), tensor: 8 (over z).
Axes of the slice: x: 4, y: 4, z: 8, core: 2. Of those that a mesh axis runs over, the one named last changes fastest.
Arguments:
- queries: bfloat16 [4096, 8192], P('seq', 'tensor'), may hold values from -6 to 6
- key_vectors: bfloat16 [4096, 8192], P('seq', 'tensor'), may hold values from -6 to 6
- value_rows: bfloat16 [4096, 8192], P('seq', 'tensor'), may hold values from -6 to 6
- gate_logits: bfloat16 [4096, 8192], P('seq', 'tensor'), may hold values from -6 to 6
- log_decay: float32 [4096, 64], P('seq', 'tensor'), may hold values from -0.73 to 0, as said below
- initial_state: float32 [64, 128, 128], P('tensor'), may hold values from -192 to 192
- norm_gain: float32 [8192], P('tensor'), may hold values from 0.25 to 1.75
- out_weight: bfloat16 [8192, 6144], P('tensor', 'seq'), may hold values from -0.0625 to 0.0625
Outputs:
- mixed: float32 [4096, 6144], P('seq', 'tensor')
Inputs may be any that keep to these rules, and one draw needn't show every extreme that they name: `log_decay`: every entry is negative.
All inputs are finite; a program needn't handle non-finite values.
Results may differ from a plain program's by a relative error of at most 0.0075.
Values may be sent and summed in bfloat16 or wider, within the bound.
No kernel may reach another device: no remote copies, remote signals or barrier semaphores. Data moves between devices by JAX's collectives and lax.ppermute only.
A program may use at most 128 MiB of HBM per device.

v0:
```python
import jax
import jax.numpy as jnp
from jax import lax
from jax.sharding import Mesh, PartitionSpec as P

HIGH = lax.Precision.HIGHEST


def entering(array, axis, combine, identity):
    length, mine = (lax.axis_size(axis), lax.axis_index(axis))
    everything = jax.tree.map(lambda part: lax.all_gather(part, axis), array)
    start = jax.tree.map(
        lambda part, zero: jnp.broadcast_to(jnp.asarray(zero, part.dtype), part.shape),
        array,
        identity,
    )

    def hop(k, before):
        reached = k < mine
        new = combine(before, jax.tree.map(lambda part: part[k], everything))
        return jax.tree.map(lambda a, b: jnp.where(reached, a, b), new, before)

    return lax.fori_loop(0, length, hop, start)


def block_step(state, pieces):
    queries_b, keys_b, values_b, decay_b = pieces
    cumulative_memory = jnp.cumsum(decay_b, axis=0)
    total = cumulative_memory[-1]
    carried = jnp.exp(cumulative_memory)[:, :, None] * jnp.einsum(
        "thd,hde->the", queries_b.astype(jnp.float32), state, precision=HIGH
    )
    scores = jnp.einsum("thd,shd->hts", queries_b, keys_b, preferred_element_type=jnp.float32)
    length = cumulative_memory.shape[0]
    lower = jnp.tril(jnp.ones((length, length), dtype=bool))[None]
    spread = cumulative_memory.T[:, :, None] - cumulative_memory.T[:, None, :]
    weights = jnp.where(lower, jnp.exp(jnp.where(lower, spread, 0.0)), 0.0)
    mixes = (scores * weights).astype(jnp.bfloat16)
    local = jnp.einsum("hts,she->the", mixes, values_b, preferred_element_type=jnp.float32)
    scaled = keys_b.astype(jnp.float32) * jnp.exp(total[None, :] - cumulative_memory)[:, :, None]
    new_state = jnp.exp(total)[:, None, None] * state + jnp.einsum(
        "shd,she->hde", scaled, values_b.astype(jnp.float32), precision=HIGH
    )
    return (new_state, carried + local)


def normalize(attended, norm_gain, gate_logits):
    mean_square = jnp.mean(attended * attended, axis=-1, keepdims=True)
    normalized_output = attended * lax.rsqrt(mean_square + 1e-05)
    flat = normalized_output.reshape(attended.shape[0], -1)
    gated = flat * norm_gain[None, :] * jax.nn.sigmoid(gate_logits.astype(jnp.float32))
    return gated.astype(jnp.bfloat16)


def chain_link(earlier, later):
    return (earlier[0] * later[0], later[0][:, None, None] * earlier[1] + later[1])


def pack(rates, state):
    heads = state.shape[0]
    flat = state.reshape(heads, -1)
    lanes = jnp.broadcast_to(rates[:, None], (heads, 128))
    return jnp.concatenate([flat, lanes], axis=1)


def link_packed(earlier, later):
    width = later.shape[1] - 128
    later_rate = later[:, width : width + 1]
    state = later_rate * earlier[:, :width] + later[:, :width]
    rate = earlier[:, width:] * later[:, width:]
    return jnp.concatenate([state, rate], axis=1)


def swap_cores(array):
    return lax.ppermute(array, "core", [(0, 1), (1, 0)])


def carried_in(rates, state, initial_state):
    chips, chip = (lax.axis_size("chip"), lax.axis_index("chip"))
    core = lax.axis_index("core")
    half = state.shape[0] // 2
    own = pack(rates, state)
    own_mine = lax.dynamic_slice_in_dim(own, core * half, half, axis=0)
    own_other = lax.dynamic_slice_in_dim(own, (1 - core) * half, half, axis=0)
    partner_mine = swap_cores(own_other)
    first_core = jnp.where(core == 0, own_mine, partner_mine)
    second_core = jnp.where(core == 0, partner_mine, own_mine)
    chip_element = link_packed(first_core, second_core)
    shifted = lax.ppermute(chip_element, "chip", [(i, i + 1) for i in range(chips - 1)])
    start_state = lax.dynamic_slice_in_dim(initial_state, core * half, half, axis=0)
    first = pack(jnp.ones((half,), rates.dtype), start_state)
    current = jnp.where(chip == 0, first, shifted)
    step = 1
    while step < chips:
        earlier = lax.ppermute(current, "chip", [(i, i + step) for i in range(chips - step)])
        current = jnp.where(chip >= step, link_packed(earlier, current), current)
        step *= 2
    for_second = link_packed(current, first_core)
    keep = jnp.where(core == 0, current, for_second)
    other = swap_cores(jnp.where(core == 0, for_second, current))
    whole = jnp.where(core == 0, jnp.concatenate([keep, other]), jnp.concatenate([other, keep]))
    width = whole.shape[1] - 128
    return whole[:, :width].reshape(state.shape)


def per_device(
    queries, key_vectors, value_rows, gate_logits, log_decay, initial_state, norm_gain, out_weight
):
    rows_here = queries.shape[0]
    head_count = log_decay.shape[1]
    head_dim = initial_state.shape[1]
    block_len = min(512, rows_here)
    block_count = rows_here // block_len

    def shaped(array):
        return array.reshape(block_count, block_len, head_count, head_dim)

    zero_state = jnp.zeros((head_count, head_dim, head_dim), jnp.float32)
    decay_blocks = log_decay.reshape(block_count, block_len, head_count)
    device_state, outputs = lax.scan(
        block_step,
        zero_state,
        (shaped(queries), shaped(key_vectors), shaped(value_rows), decay_blocks),
    )
    local_out = outputs.reshape(rows_here, head_count, head_dim)
    through = jnp.cumsum(log_decay, axis=0)
    shard_fading_rates = jnp.exp(through[-1])
    incoming = carried_in(shard_fading_rates, device_state, initial_state)
    query_float = queries.reshape(rows_here, head_count, head_dim).astype(jnp.float32)
    inherited = jnp.exp(through)[:, :, None] * jnp.einsum(
        "thd,hde->the", query_float, incoming, precision=HIGH
    )
    attended = local_out + inherited
    hidden = normalize(attended, norm_gain, gate_logits)
    terms = jnp.dot(
        hidden,
        lax.all_gather(out_weight, ("chip", "core"), axis=1, tiled=True),
        preferred_element_type=jnp.float32,
    )
    mixed = lax.psum_scatter(terms, "tensor", scatter_dimension=1, tiled=True)
    return mixed


def solution(mesh):
    seq_len, groups = mesh.devices.shape
    split = Mesh(mesh.devices.reshape(seq_len // 2, 2, groups), ("chip", "core", "tensor"))
    tokens = ("chip", "core")
    return jax.shard_map(
        per_device,
        mesh=split,
        in_specs=(
            P(tokens, "tensor"),
            P(tokens, "tensor"),
            P(tokens, "tensor"),
            P(tokens, "tensor"),
            P(tokens, "tensor"),
            P("tensor", None, None),
            P("tensor"),
            P("tensor", tokens),
        ),
        out_specs=P(tokens, "tensor"),
        check_vma=False,
    )
```

profile of v0, /device:TPU:14, one launch (start us, length us, event | category | flops | bytes accessed | tf_op | source)
XLA Modules:
  0.0 184.1 jit_solution(1943625744013885073)
XLA Ops:
  6.6 0.9 copy.35
  7.5 0.2 reduce_window_sum.13
  7.8 1.1 copy.52
  8.9 1.4 fusion.4
  10.3 0.3 copy.89
  10.6 0.1 broadcast_in_dim.56
  10.7 0.1 collective-permute-start
  10.8 1.5 collective-permute-done
  12.3 0.1 broadcast_select_fusion
  12.4 0.1 slice_reduce_fusion.5
  12.6 0.2 slice_add_fusion.4
  12.8 3.4 %collective-permute-start.1 = (f32[4,16512]{1,0:T(4,128)S(1)}, f32[4,16512]{1,0:T(4,128)S(1)}, u32[]{:S(2)}, u32[]{:S(2)}) collective-permute-start(f32[4,16512]{1,0:T(4,128)S(1)} %pad_maximum_fusion.2), channel_id=1, source_target_pairs={{0,16},{16,32},{32,48},{48,64},{64,80},{80,96},{96,112},{112,128},... | collective-permute-start | bytes 792584 | tf_op jit(solution)/shard_map/ppermute | solution.py:89
  16.2 0.2 copy.90
  16.4 6.6 %collective-permute-done.1 = f32[4,16512]{1,0:T(4,128)S(1)} collective-permute-done((f32[4,16512]{1,0:T(4,128)S(1)}, f32[4,16512]{1,0:T(4,128)S(1)}, u32[]{:S(2)}, u32[]{:S(2)}) %collective-permute-start.1) | collective-permute-done | bytes 264224 | tf_op jit(solution)/shard_map/ppermute | solution.py:89
  23.1 0.1 pad_select_fusion
  23.1 5.5 %collective-permute-start.2 = (f32[4,16512]{1,0:T(4,128)S(1)}, f32[4,16512]{1,0:T(4,128)S(1)}, u32[]{:S(2)}, u32[]{:S(2)}) collective-permute-start(f32[4,16512]{1,0:T(4,128)S(1)} %pad_select_fusion), channel_id=1, source_target_pairs={{0,16},{16,32},{32,48},{48,64},{64,80},{80,96},{96,112},{112,128},... | collective-permute-start | bytes 792584 | tf_op jit(solution)/shard_map/ppermute | solution.py:95
  28.7 0.1 slice_reduce_fusion.4
  28.8 4.9 %collective-permute-done.2 = f32[4,16512]{1,0:T(4,128)S(1)} collective-permute-done((f32[4,16512]{1,0:T(4,128)S(1)}, f32[4,16512]{1,0:T(4,128)S(1)}, u32[]{:S(2)}, u32[]{:S(2)}) %collective-permute-start.2) | collective-permute-done | bytes 264224 | tf_op jit(solution)/shard_map/ppermute | solution.py:95
  33.7 0.1 slice_add_fusion.3
  33.8 0.1 maximum_select_fusion
  33.9 4.1 %collective-permute-start.3 = (f32[4,16512]{1,0:T(4,128)S(1)}, f32[4,16512]{1,0:T(4,128)S(1)}, u32[]{:S(2)}, u32[]{:S(2)}) collective-permute-start(f32[4,16512]{1,0:T(4,128)S(1)} %maximum_select_fusion), channel_id=1, source_target_pairs={{0,32},{16,48},{32,64},{48,80},{64,96},{80,112},{96,128},{112,144}... | collective-permute-start | bytes 792584 | tf_op jit(solution)/shard_map/ppermute | solution.py:95
  38.1 0.1 slice_reduce_fusion.3
  38.2 5.8 %collective-permute-done.3 = f32[4,16512]{1,0:T(4,128)S(1)} collective-permute-done((f32[4,16512]{1,0:T(4,128)S(1)}, f32[4,16512]{1,0:T(4,128)S(1)}, u32[]{:S(2)}, u32[]{:S(2)}) %collective-permute-start.3) | collective-permute-done | bytes 264224 | tf_op jit(solution)/shard_map/ppermute | solution.py:95
  44.0 0.1 slice_add_fusion.2
  44.2 0.1 maximum_select_fusion.1
  44.3 3.2 %collective-permute-start.4 = (f32[4,16512]{1,0:T(4,128)S(1)}, f32[4,16512]{1,0:T(4,128)S(1)}, u32[]{:S(2)}, u32[]{:S(2)}) collective-permute-start(f32[4,16512]{1,0:T(4,128)S(1)} %maximum_select_fusion.1), channel_id=1, source_target_pairs={{0,64},{16,80},{32,96},{48,112},{64,128},{80,144},{96,160},{112,17... | collective-permute-start | bytes 792584 | tf_op jit(solution)/shard_map/ppermute | solution.py:95
  47.5 0.1 slice_reduce_fusion.2
  47.6 4.9 %collective-permute-done.4 = f32[4,16512]{1,0:T(4,128)S(1)} collective-permute-done((f32[4,16512]{1,0:T(4,128)S(1)}, f32[4,16512]{1,0:T(4,128)S(1)}, u32[]{:S(2)}, u32[]{:S(2)}) %collective-permute-start.4) | collective-permute-done | bytes 264224 | tf_op jit(solution)/shard_map/ppermute | solution.py:95
  52.5 0.1 slice_add_fusion.1
  52.7 0.1 maximum_select_fusion.2
  52.8 3.1 %collective-permute-start.5 = (f32[4,16512]{1,0:T(4,128)S(1)}, f32[4,16512]{1,0:T(4,128)S(1)}, u32[]{:S(2)}, u32[]{:S(2)}) collective-permute-start(f32[4,16512]{1,0:T(4,128)S(1)} %maximum_select_fusion.2), channel_id=1, source_target_pairs={{0,128},{16,144},{32,160},{48,176},{64,192},{80,208},{96,224},{112... | collective-permute-start | bytes 792584 | tf_op jit(solution)/shard_map/ppermute | solution.py:95
  55.9 0.1 slice_reduce_fusion
  56.0 0.1 slice_reduce_fusion.1
  56.1 3.6 %collective-permute-done.5 = f32[4,16512]{1,0:T(4,128)S(1)} collective-permute-done((f32[4,16512]{1,0:T(4,128)S(1)}, f32[4,16512]{1,0:T(4,128)S(1)}, u32[]{:S(2)}, u32[]{:S(2)}) %collective-permute-start.5) | collective-permute-done | bytes 264224 | tf_op jit(solution)/shard_map/ppermute | solution.py:95
  59.8 0.1 slice_add_fusion
  59.9 0.1 maximum_select_fusion.3
  60.0 0.1 fusion.25
  60.2 0.1 fusion.41
  60.3 0.1 collective-permute-start.6
  60.5 0.7 fusion.2
  61.2 0.7 collective-permute-done.6
  61.9 0.2 fusion.9
  62.1 0.6 fusion.3
  62.7 0.5 multiply_reduce_fusion
  63.3 0.2 copy.49
  63.5 54.9 %all-gather.2.cloned.1.call-done = bf16[1024,6144]{0,1:T(8,128)(2,1)} async-done(((bf16[1024,192]{0,1:T(8,128)(2,1)}), bf16[1024,6144]{0,1:T(8,128)(2,1)}) %all-gather.2.cloned.1.call-update) | async-done | bytes 12582928 | tf_op jit(solution)/shard_map/all_gather | solution.py:137
  118.4 10.5 %fusion.18 = f32[128,6144]{1,0:T(8,128)} fusion(bf16[1024,6144]{0,1:T(8,128)(2,1)} %all-gather.2.cloned.1.call-done, bf16[128,1024]{1,0:T(8,128)(2,1)S(1)} %copy-done.3, f32[128,1024]{1,0:T(8,128)S(1)} %copy.49, f32[1024]{0:T(1024)S(1)} %copy-done.4), kind=kOutput, calls=%fused_computation.39 | convolution fusion | flops 1611530240 | bytes 16519168 | tf_op jit(solution)/shard_map/dot_general | solution.py:135
  128.9 48.3 %reduce-scatter.2.cloned.1.call-done = f32[128,768]{1,0:T(8,128)} async-done(((f32[128,6144]{1,0:T(8,128)}), f32[128,768]{1,0:T(8,128)}) %reduce-scatter.2.cloned.1.call-update) | async-done | bytes 393232 | tf_op jit(solution)/shard_map/reduce_scatter | solution.py:140
  (32 shorter events, 0.6 us)
Async XLA Ops:
  6.5 9.7 %copy-start = (f32[8,128,128]{2,1,0:T(8,128)S(1)}, f32[8,128,128]{2,1,0:T(8,128)}, u32[]{:S(2)}) copy-start(f32[8,128,128]{2,1,0:T(8,128)} %param.13) | copy-start | bytes 1572868
  6.5 56.2 %copy-start.2 = (bf16[128,1024]{1,0:T(8,128)(2,1)S(1)}, bf16[128,1024]{1,0:T(8,128)(2,1)}, u32[]{:S(2)}) copy-start(bf16[128,1024]{1,0:T(8,128)(2,1)} %param.10) | copy-start | bytes 786436
  6.5 54.0 %copy-start.1 = (bf16[128,1024]{1,0:T(8,128)(2,1)S(1)}, bf16[128,1024]{1,0:T(8,128)(2,1)}, u32[]{:S(2)}) copy-start(bf16[128,1024]{1,0:T(8,128)(2,1)} %param.8) | copy-start | bytes 786436
  6.5 111.9 %copy-start.4 = (f32[1024]{0:T(1024)S(1)}, f32[1024]{0:T(1024)}, u32[]{:S(2)}) copy-start(f32[1024]{0:T(1024)} %param.14) | copy-start | bytes 12292
  6.5 111.9 %copy-start.3 = (bf16[128,1024]{1,0:T(8,128)(2,1)S(1)}, bf16[128,1024]{1,0:T(8,128)(2,1)}, u32[]{:S(2)}) copy-start(bf16[128,1024]{1,0:T(8,128)(2,1)} %param.11) | copy-start | bytes 786436
  6.5 111.9 %all-gather.2.cloned.1.call-start = ((), (), s32[]{:S(2)}) async-start(), calls=%async_computation.1 | async-start | bytes 12976128 | tf_op jit(solution)/shard_map/all_gather | solution.py:137
  10.7 1.6 collective-permute-start
  12.8 10.3 %collective-permute-start.1 = (f32[4,16512]{1,0:T(4,128)S(1)}, f32[4,16512]{1,0:T(4,128)S(1)}, u32[]{:S(2)}, u32[]{:S(2)}) collective-permute-start(f32[4,16512]{1,0:T(4,128)S(1)} %pad_maximum_fusion.2), channel_id=1, source_target_pairs={{0,16},{16,32},{32,48},{48,64},{64,80},{80,96},{96,112},{112,128},... | collective-permute-start | bytes 792584 | tf_op jit(solution)/shard_map/ppermute | solution.py:89
  23.1 10.5 %collective-permute-start.2 = (f32[4,16512]{1,0:T(4,128)S(1)}, f32[4,16512]{1,0:T(4,128)S(1)}, u32[]{:S(2)}, u32[]{:S(2)}) collective-permute-start(f32[4,16512]{1,0:T(4,128)S(1)} %pad_select_fusion), channel_id=1, source_target_pairs={{0,16},{16,32},{32,48},{48,64},{64,80},{80,96},{96,112},{112,128},... | collective-permute-start | bytes 792584 | tf_op jit(solution)/shard_map/ppermute | solution.py:95
  33.9 10.1 %collective-permute-start.3 = (f32[4,16512]{1,0:T(4,128)S(1)}, f32[4,16512]{1,0:T(4,128)S(1)}, u32[]{:S(2)}, u32[]{:S(2)}) collective-permute-start(f32[4,16512]{1,0:T(4,128)S(1)} %maximum_select_fusion), channel_id=1, source_target_pairs={{0,32},{16,48},{32,64},{48,80},{64,96},{80,112},{96,128},{112,144}... | collective-permute-start | bytes 792584 | tf_op jit(solution)/shard_map/ppermute | solution.py:95
  44.3 8.3 %collective-permute-start.4 = (f32[4,16512]{1,0:T(4,128)S(1)}, f32[4,16512]{1,0:T(4,128)S(1)}, u32[]{:S(2)}, u32[]{:S(2)}) collective-permute-start(f32[4,16512]{1,0:T(4,128)S(1)} %maximum_select_fusion.1), channel_id=1, source_target_pairs={{0,64},{16,80},{32,96},{48,112},{64,128},{80,144},{96,160},{112,17... | collective-permute-start | bytes 792584 | tf_op jit(solution)/shard_map/ppermute | solution.py:95
  47.5 129.8 %reduce-scatter.2.cloned.1.call-start = ((), (), s32[]{:S(2)}) async-start(), calls=%async_computation.2 | async-start | bytes 3538944 | tf_op jit(solution)/shard_map/reduce_scatter | solution.py:140
  52.8 7.0 %collective-permute-start.5 = (f32[4,16512]{1,0:T(4,128)S(1)}, f32[4,16512]{1,0:T(4,128)S(1)}, u32[]{:S(2)}, u32[]{:S(2)}) collective-permute-start(f32[4,16512]{1,0:T(4,128)S(1)} %maximum_select_fusion.2), channel_id=1, source_target_pairs={{0,128},{16,144},{32,160},{48,176},{64,192},{80,208},{96,224},{112... | collective-permute-start | bytes 792584 | tf_op jit(solution)/shard_map/ppermute | solution.py:95
  60.3 1.6 collective-permute-start.6
Sparse Core Ops, SparseCore 0:
  47.6 70.7 all-gather.1
  129.0 48.1 reduce-scatter.1
where the time goes:
time: 184 us
  waiting for transfers between devices  131 us (71%)
  starting transfers between devices  19.6 us (11%)
  between operations  13.7 us (7%)
  matrix products  13.6 us (7%)
  local copies, waits for them, and re-layouts  3.67 us (2%)
  other arithmetic  2.07 us (1%)
    all_gather x1, waiting for transfers between devices, per_device(): lax.all_gather(out_weight, ('chip', 'core'), axis=1, tiled=True)  54.9 us
    reduce_scatter x1, waiting for transfers between devices, per_device(): mixed = lax.psum_scatter(terms, 'tensor', scatter_dimension=1, tiled=True)  48.3 us
    ppermute x4, waiting for transfers between devices, carried_in(): lax.ppermute(current, 'chip', [(i, i + step) for i in range(chips - step)])  19.3 us
    ppermute x4, starting transfers between devices, carried_in(): lax.ppermute(current, 'chip', [(i, i + step) for i in range(chips - step)])  15.9 us
    dot_general x1, matrix products, per_device(): jnp.dot(hidden, lax.all_gather(out_weight, ('chip', 'core'), axis=1, tile...  10.5 us
    ppermute x1, waiting for transfers between devices, carried_in(): lax.ppermute(chip_element, 'chip', [(i, i + 1) for i in range(chips - 1)])  6.65 us
  transfers between devices with their start and end apart: 9, of which 9 were waited for; matrix products, arithmetic and copies ran while one was open for 2% of the time, Pallas kernels for 0%

commit v1 on v0

--- a/solution.py
+++ b/solution.py
@@ -106,6 +106,15 @@
 def per_device(
     queries, key_vectors, value_rows, gate_logits, log_decay, initial_state, norm_gain, out_weight
 ):
+
+    def touch_arrays_on(q_in):
+        return jnp.concatenate(
+            lax.all_to_all(
+                jnp.stack([q_in] * lax.axis_size(("chip", "core"))), ("chip", "core"), 0, 0
+            ),
+            axis=1,
+        )
+
     rows_here = queries.shape[0]
     head_count = log_decay.shape[1]
     head_dim = initial_state.shape[1]
@@ -132,11 +141,7 @@
     )
     attended = local_out + inherited
     hidden = normalize(attended, norm_gain, gate_logits)
-    terms = jnp.dot(
-        hidden,
-        lax.all_gather(out_weight, ("chip", "core"), axis=1, tiled=True),
-        preferred_element_type=jnp.float32,
-    )
+    terms = jnp.dot(hidden, touch_arrays_on(out_weight), preferred_element_type=jnp.float32)
     mixed = lax.psum_scatter(terms, "tensor", scatter_dimension=1, tiled=True)
     return mixed
 

time: 184 us -> 297 us (1.61)
  waiting for transfers between devices: 131 us -> 226 us
  starting transfers between devices: 19.6 us -> 30.9 us
  local copies, waits for them, and re-layouts: 3.67 us -> 9.73 us
    all_to_all x0 -> x1, waiting for transfers between devices: none -> 141 us  [touch_arrays_on(): lax.all_to_all(jnp.stack([q_in] * lax.axis_size(('chip', 'core'))), ('chi...]
    all_gather x1 -> x0, waiting for transfers between devices: 54.9 us -> none  [per_device(): lax.all_gather(out_weight, ('chip', 'core'), axis=1, tiled=True)]
    reduce_scatter x1, waiting for transfers between devices: 48.3 us -> 60.8 us  [per_device(): mixed = lax.psum_scatter(terms, 'tensor', scatter_dimension=1, tiled=True)]
    all_to_all x0 -> x1, starting transfers between devices: none -> 11.2 us  [touch_arrays_on(): lax.all_to_all(jnp.stack([q_in] * lax.axis_size(('chip', 'core'))), ('chi...]
    another operation x0 -> x1, local copies, waits for them, and re-layouts: none -> 6.09 us  [touch_arrays_on(): jnp.stack([q_in] * lax.axis_size(('chip', 'core')))]
    ppermute x4, waiting for transfers between devices: 19.3 us -> 15.7 us  [carried_in(): lax.ppermute(current, 'chip', [(i, i + step) for i in range(chips - step)])]
  transfers between devices with their start and end apart: 9 -> 9, of which waited for: 9 -> 8; matrix products, arithmetic and copies ran while one was open for 2% -> 3% of each run, Pallas kernels for 0% -> 0%
where the time goes in v1:
time: 297 us; the launch traced here: 296 us
  waiting for transfers between devices  226 us (76%)
  starting transfers between devices  30.9 us (10%)
  between operations  13.7 us (5%)
  matrix products  13.6 us (5%)
  local copies, waits for them, and re-layouts  9.73 us (3%)
    all_to_all x1, waiting for transfers between devices, touch_arrays_on(): lax.all_to_all(jnp.stack([q_in] * lax.axis_size(('chip', 'core'))), ('chi...  141 us
    reduce_scatter x1, waiting for transfers between devices, per_device(): mixed = lax.psum_scatter(terms, 'tensor', scatter_dimension=1, tiled=True)  60.8 us
    ppermute x4, starting transfers between devices, carried_in(): lax.ppermute(current, 'chip', [(i, i + step) for i in range(chips - step)])  15.9 us
    ppermute x4, waiting for transfers between devices, carried_in(): lax.ppermute(current, 'chip', [(i, i + step) for i in range(chips - step)])  15.7 us
    all_to_all x1, starting transfers between devices, touch_arrays_on(): lax.all_to_all(jnp.stack([q_in] * lax.axis_size(('chip', 'core'))), ('chi...  11.2 us
    dot_general x1, matrix products, per_device(): jnp.dot(hidden, touch_arrays_on(out_weight), preferred_element_type=jnp.f...  10.4 us
    ppermute x1, waiting for transfers between devices, carried_in(): lax.ppermute(chip_element, 'chip', [(i, i + 1) for i in range(chips - 1)])  6.65 us
    another operation x1, local copies, waits for them, and re-layouts, touch_arrays_on(): jnp.stack([q_in] * lax.axis_size(('chip', 'core')))  6.09 us
  transfers between devices with their start and end apart: 9, of which 8 were waited for; matrix products, arithmetic and copies ran while one was open for 3% of the time, Pallas kernels for 0%

profile of v1, /device:TPU:14, one launch (start us, length us, event | category | flops | bytes accessed | tf_op | source)
XLA Modules:
  0.0 296.1 jit_solution(13179666561960264411)
XLA Ops:
  6.5 0.9 copy.36
  7.4 0.2 reduce_window_sum.13
  7.6 1.1 copy.53
  8.8 1.4 fusion.4
  10.2 0.3 copy.90
  10.6 0.1 collective-permute-start
  10.7 1.5 collective-permute-done
  12.3 0.1 broadcast_select_fusion
  12.4 0.1 slice_reduce_fusion.5
  12.5 0.2 slice_add_fusion.4
  12.7 3.4 %collective-permute-start.1 = (f32[4,16512]{1,0:T(4,128)S(1)}, f32[4,16512]{1,0:T(4,128)S(1)}, u32[]{:S(2)}, u32[]{:S(2)}) collective-permute-start(f32[4,16512]{1,0:T(4,128)S(1)} %pad_maximum_fusion.2), channel_id=1, source_target_pairs={{0,16},{16,32},{32,48},{48,64},{64,80},{80,96},{96,112},{112,128},... | collective-permute-start | bytes 792584 | tf_op jit(solution)/shard_map/ppermute | solution.py:89
  16.2 0.2 copy.91
  16.3 6.6 %collective-permute-done.1 = f32[4,16512]{1,0:T(4,128)S(1)} collective-permute-done((f32[4,16512]{1,0:T(4,128)S(1)}, f32[4,16512]{1,0:T(4,128)S(1)}, u32[]{:S(2)}, u32[]{:S(2)}) %collective-permute-start.1) | collective-permute-done | bytes 264224 | tf_op jit(solution)/shard_map/ppermute | solution.py:89
  23.0 0.1 pad_select_fusion
  23.1 5.5 %collective-permute-start.2 = (f32[4,16512]{1,0:T(4,128)S(1)}, f32[4,16512]{1,0:T(4,128)S(1)}, u32[]{:S(2)}, u32[]{:S(2)}) collective-permute-start(f32[4,16512]{1,0:T(4,128)S(1)} %pad_select_fusion), channel_id=1, source_target_pairs={{0,16},{16,32},{32,48},{48,64},{64,80},{80,96},{96,112},{112,128},... | collective-permute-start | bytes 792584 | tf_op jit(solution)/shard_map/ppermute | solution.py:95
  28.6 0.1 slice_reduce_fusion.4
  28.7 4.9 %collective-permute-done.2 = f32[4,16512]{1,0:T(4,128)S(1)} collective-permute-done((f32[4,16512]{1,0:T(4,128)S(1)}, f32[4,16512]{1,0:T(4,128)S(1)}, u32[]{:S(2)}, u32[]{:S(2)}) %collective-permute-start.2) | collective-permute-done | bytes 264224 | tf_op jit(solution)/shard_map/ppermute | solution.py:95
  33.6 0.1 slice_add_fusion.3
  33.8 0.1 maximum_select_fusion
  33.9 4.1 %collective-permute-start.3 = (f32[4,16512]{1,0:T(4,128)S(1)}, f32[4,16512]{1,0:T(4,128)S(1)}, u32[]{:S(2)}, u32[]{:S(2)}) collective-permute-start(f32[4,16512]{1,0:T(4,128)S(1)} %maximum_select_fusion), channel_id=1, source_target_pairs={{0,32},{16,48},{32,64},{48,80},{64,96},{80,112},{96,128},{112,144}... | collective-permute-start | bytes 792584 | tf_op jit(solution)/shard_map/ppermute | solution.py:95
  38.0 0.1 slice_reduce_fusion.3
  38.1 5.8 %collective-permute-done.3 = f32[4,16512]{1,0:T(4,128)S(1)} collective-permute-done((f32[4,16512]{1,0:T(4,128)S(1)}, f32[4,16512]{1,0:T(4,128)S(1)}, u32[]{:S(2)}, u32[]{:S(2)}) %collective-permute-start.3) | collective-permute-done | bytes 264224 | tf_op jit(solution)/shard_map/ppermute | solution.py:95
  44.0 0.1 slice_add_fusion.2
  44.1 0.1 maximum_select_fusion.1
  44.2 3.2 %collective-permute-start.4 = (f32[4,16512]{1,0:T(4,128)S(1)}, f32[4,16512]{1,0:T(4,128)S(1)}, u32[]{:S(2)}, u32[]{:S(2)}) collective-permute-start(f32[4,16512]{1,0:T(4,128)S(1)} %maximum_select_fusion.1), channel_id=1, source_target_pairs={{0,64},{16,80},{32,96},{48,112},{64,128},{80,144},{96,160},{112,17... | collective-permute-start | bytes 792584 | tf_op jit(solution)/shard_map/ppermute | solution.py:95
  47.4 0.1 slice_reduce_fusion.2
  47.5 5.0 %collective-permute-done.4 = f32[4,16512]{1,0:T(4,128)S(1)} collective-permute-done((f32[4,16512]{1,0:T(4,128)S(1)}, f32[4,16512]{1,0:T(4,128)S(1)}, u32[]{:S(2)}, u32[]{:S(2)}) %collective-permute-start.4) | collective-permute-done | bytes 264224 | tf_op jit(solution)/shard_map/ppermute | solution.py:95
  52.5 0.1 slice_add_fusion.1
  52.6 0.1 maximum_select_fusion.2
  52.7 3.1 %collective-permute-start.5 = (f32[4,16512]{1,0:T(4,128)S(1)}, f32[4,16512]{1,0:T(4,128)S(1)}, u32[]{:S(2)}, u32[]{:S(2)}) collective-permute-start(f32[4,16512]{1,0:T(4,128)S(1)} %maximum_select_fusion.2), channel_id=1, source_target_pairs={{0,128},{16,144},{32,160},{48,176},{64,192},{80,208},{96,224},{112... | collective-permute-start | bytes 792584 | tf_op jit(solution)/shard_map/ppermute | solution.py:95
  55.8 6.1 %stack.2 = bf16[32,1024,192]{1,2,0:T(8,128)(2,1)} broadcast(bf16[1024,192]{0,1:T(8,128)(2,1)S(1)} %copy-done.3), dimensions={1,2} | broadcast | bytes 12976128 | tf_op jit(solution)/shard_map/stack | solution.py:113
  61.9 11.2 %all-to-all-start = ((bf16[32,1024,192]{1,2,0:T(8,128)(2,1)}), bf16[32,1024,192]{1,2,0:T(8,128)(2,1)}, u32[]{:S(2)}, u32[]{:S(2)}) async-start(bf16[32,1024,192]{1,2,0:T(8,128)(2,1)} %stack.2), calls=%async_computation | async-start | bytes 25165824 | tf_op jit(solution)/shard_map/all_to_all | solution.py:112
  73.2 0.1 slice_reduce_fusion
  73.4 0.1 slice_reduce_fusion.1
  73.5 0.1 slice_add_fusion
  73.6 0.1 maximum_select_fusion.3
  73.7 0.1 fusion.25
  73.9 0.1 fusion.41
  74.0 0.2 collective-permute-start.6
  74.3 0.7 fusion.2
  75.0 0.6 collective-permute-done.6
  75.6 0.2 fusion.9
  75.8 0.6 fusion.3
  76.4 0.5 multiply_reduce_fusion
  77.0 0.2 copy.50
  77.2 140.7 %all-to-all-done = bf16[32,1024,192]{1,2,0:T(8,128)(2,1)} async-done(((bf16[32,1024,192]{1,2,0:T(8,128)(2,1)}), bf16[32,1024,192]{1,2,0:T(8,128)(2,1)}, u32[]{:S(2)}, u32[]{:S(2)}) %all-to-all-start) | async-done | bytes 12582944 | tf_op jit(solution)/shard_map/all_to_all | solution.py:112
  217.9 10.4 %fusion.18 = f32[128,6144]{1,0:T(8,128)} fusion(bf16[1024,6144]{0,1:T(8,128)(2,1)} %bitcast.7, bf16[128,1024]{1,0:T(8,128)(2,1)S(1)} %copy-done.4, f32[128,1024]{1,0:T(8,128)S(1)} %copy.50, f32[1024]{0:T(1024)S(1)} %copy-done.5), kind=kOutput, calls=%fused_computation.39 | convolution fusion | flops 1611530240 | bytes 16519168 | tf_op jit(solution)/shard_map/dot_general | solution.py:144
  228.4 60.8 %reduce-scatter.2.cloned.1.call-done = f32[128,768]{1,0:T(8,128)} async-done(((f32[128,6144]{1,0:T(8,128)}), f32[128,768]{1,0:T(8,128)}) %reduce-scatter.2.cloned.1.call-update) | async-done | bytes 393232 | tf_op jit(solution)/shard_map/reduce_scatter | solution.py:145
  (34 shorter events, 0.6 us)
Async XLA Ops:
  6.5 9.6 %copy-start = (f32[8,128,128]{2,1,0:T(8,128)S(1)}, f32[8,128,128]{2,1,0:T(8,128)}, u32[]{:S(2)}) copy-start(f32[8,128,128]{2,1,0:T(8,128)} %param.13) | copy-start | bytes 1572868
  6.5 49.3 %copy-start.3 = (bf16[1024,192]{0,1:T(8,128)(2,1)S(1)}, bf16[1024,192]{0,1:T(8,128)(2,1)}, u32[]{:S(2)}) copy-start(bf16[1024,192]{0,1:T(8,128)(2,1)} %param.15) | copy-start | bytes 1179652
  10.6 1.6 collective-permute-start
  12.7 10.3 %collective-permute-start.1 = (f32[4,16512]{1,0:T(4,128)S(1)}, f32[4,16512]{1,0:T(4,128)S(1)}, u32[]{:S(2)}, u32[]{:S(2)}) collective-permute-start(f32[4,16512]{1,0:T(4,128)S(1)} %pad_maximum_fusion.2), channel_id=1, source_target_pairs={{0,16},{16,32},{32,48},{48,64},{64,80},{80,96},{96,112},{112,128},... | collective-permute-start | bytes 792584 | tf_op jit(solution)/shard_map/ppermute | solution.py:89
  23.1 10.5 %collective-permute-start.2 = (f32[4,16512]{1,0:T(4,128)S(1)}, f32[4,16512]{1,0:T(4,128)S(1)}, u32[]{:S(2)}, u32[]{:S(2)}) collective-permute-start(f32[4,16512]{1,0:T(4,128)S(1)} %pad_select_fusion), channel_id=1, source_target_pairs={{0,16},{16,32},{32,48},{48,64},{64,80},{80,96},{96,112},{112,128},... | collective-permute-start | bytes 792584 | tf_op jit(solution)/shard_map/ppermute | solution.py:95
  33.9 10.1 %collective-permute-start.3 = (f32[4,16512]{1,0:T(4,128)S(1)}, f32[4,16512]{1,0:T(4,128)S(1)}, u32[]{:S(2)}, u32[]{:S(2)}) collective-permute-start(f32[4,16512]{1,0:T(4,128)S(1)} %maximum_select_fusion), channel_id=1, source_target_pairs={{0,32},{16,48},{32,64},{48,80},{64,96},{80,112},{96,128},{112,144}... | collective-permute-start | bytes 792584 | tf_op jit(solution)/shard_map/ppermute | solution.py:95
  44.2 8.3 %collective-permute-start.4 = (f32[4,16512]{1,0:T(4,128)S(1)}, f32[4,16512]{1,0:T(4,128)S(1)}, u32[]{:S(2)}, u32[]{:S(2)}) collective-permute-start(f32[4,16512]{1,0:T(4,128)S(1)} %maximum_select_fusion.1), channel_id=1, source_target_pairs={{0,64},{16,80},{32,96},{48,112},{64,128},{80,144},{96,160},{112,17... | collective-permute-start | bytes 792584 | tf_op jit(solution)/shard_map/ppermute | solution.py:95
  52.7 20.8 %collective-permute-start.5 = (f32[4,16512]{1,0:T(4,128)S(1)}, f32[4,16512]{1,0:T(4,128)S(1)}, u32[]{:S(2)}, u32[]{:S(2)}) collective-permute-start(f32[4,16512]{1,0:T(4,128)S(1)} %maximum_select_fusion.2), channel_id=1, source_target_pairs={{0,128},{16,144},{32,160},{48,176},{64,192},{80,208},{96,224},{112... | collective-permute-start | bytes 792584 | tf_op jit(solution)/shard_map/ppermute | solution.py:95
  61.9 12.4 %copy-start.1 = (bf16[128,1024]{1,0:T(8,128)(2,1)S(1)}, bf16[128,1024]{1,0:T(8,128)(2,1)}, u32[]{:S(2)}) copy-start(bf16[128,1024]{1,0:T(8,128)(2,1)} %param.8) | copy-start | bytes 786436
  61.9 14.5 %copy-start.2 = (bf16[128,1024]{1,0:T(8,128)(2,1)S(1)}, bf16[128,1024]{1,0:T(8,128)(2,1)}, u32[]{:S(2)}) copy-start(bf16[128,1024]{1,0:T(8,128)(2,1)} %param.10) | copy-start | bytes 786436
  61.9 156.0 %copy-start.4 = (bf16[128,1024]{1,0:T(8,128)(2,1)S(1)}, bf16[128,1024]{1,0:T(8,128)(2,1)}, u32[]{:S(2)}) copy-start(bf16[128,1024]{1,0:T(8,128)(2,1)} %param.11) | copy-start | bytes 786436
  61.9 156.0 %copy-start.5 = (f32[1024]{0:T(1024)S(1)}, f32[1024]{0:T(1024)}, u32[]{:S(2)}) copy-start(f32[1024]{0:T(1024)} %param.14) | copy-start | bytes 12292
  61.9 156.0 %all-to-all-start = ((bf16[32,1024,192]{1,2,0:T(8,128)(2,1)}), bf16[32,1024,192]{1,2,0:T(8,128)(2,1)}, u32[]{:S(2)}, u32[]{:S(2)}) async-start(bf16[32,1024,192]{1,2,0:T(8,128)(2,1)} %stack.2), calls=%async_computation | async-start | bytes 25165824 | tf_op jit(solution)/shard_map/all_to_all | solution.py:112
  73.2 216.1 %reduce-scatter.2.cloned.1.call-start = ((), (), s32[]{:S(2)}) async-start(), calls=%async_computation.2 | async-start | bytes 3538944 | tf_op jit(solution)/shard_map/reduce_scatter | solution.py:145
  74.0 1.6 collective-permute-start.6
Sparse Core Ops, SparseCore 0:
  228.5 60.6 reduce-scatter.1
